TPU v7x, 32 devices: a whole 2x2x4 slice. The times are simulated.
32 devices in a mesh: groups: 2 (over y), hid: 4 (over z), rows: 2 (over x), mp: 2 (over core).
Axes of the slice: x: 2, y: 2, z: 4, core: 2. Of those that a mesh axis runs over, the one named last changes fastest.
Arguments:
- tokens: bfloat16 [1024, 4096], P(('groups', 'rows'), 'hid'), parts along dimension 0, may hold values from -6 to 6
- norm_gain: float32 [2, 4096], P('mp'), may hold values from 0.1 to 1.9
- gate_weight: bfloat16 [2, 4096, 14336], P('mp', 'rows', 'hid'), may hold values from -0.09375 to 0.09375
- up_weight: bfloat16 [2, 4096, 14336], P('mp', 'rows', 'hid'), may hold values from -0.09375 to 0.09375
- down_weight: bfloat16 [2, 14336, 4096], P('mp', 'hid', 'rows'), may hold values from -0.046875 to 0.046875
- enc_weight: bfloat16 [2, 4096, 16384], P('mp', 'rows', 'hid'), may hold values from -0.0625 to 0.0625
- enc_bias: float32 [16384], P('hid'), may hold values from -3 to 3
- adjoint: bfloat16 [1024, 16384], P(('groups', 'rows', 'mp'), 'hid'), parts along dimension 0, may hold values from -6 to 6
Outputs:
- gated: bfloat16 [1024, 16384], P(('groups', 'rows', 'mp'), 'hid'), parts along dimension 0
There are 2 independent parts, one for each index of `groups`. A program takes and returns all parts, laid end to end along the dimension named above; an argument that names none is the same for every part. Nothing has to cross between parts.
All inputs are finite; a program needn't handle non-finite values.
Results may differ from a plain program's by a relative error of at most 0.0058.
Values may be sent and summed in bfloat16 or wider, within the bound.
A program may use at most 128 MiB of HBM per device.

v0:
```python
import jax
import jax.numpy as jnp
from jax import lax
from jax.sharding import PartitionSpec as P


def on_device(
    tokens, norm_gain, gate_weight, up_weight, down_weight, enc_weight, enc_bias, adjoint
):
    gathered = lax.all_gather(tokens, "hid", axis=1, tiled=True)
    tokens_float = gathered.astype(jnp.float32)
    inverse_rms = lax.rsqrt(jnp.mean(tokens_float * tokens_float, axis=-1, keepdims=True) + 1e-05)
    normed = (tokens_float * inverse_rms * norm_gain[0][None, :]).astype(jnp.bfloat16)
    gate_local = gate_weight[0]
    up_local = up_weight[0]
    hidden_width = gate_local.shape[1]
    all_normed = lax.all_gather(normed, "rows", axis=0, tiled=True)
    width_rows = gate_local.shape[0]
    column_start = lax.axis_index("rows") * width_rows
    own_columns = lax.dynamic_slice_in_dim(all_normed, column_start, width_rows, 1)
    both_local = jnp.concatenate((gate_local, up_local), axis=1)
    selected = own_columns
    summed = lax.psum_scatter(
        jnp.dot(selected, both_local, preferred_element_type=jnp.float32),
        "rows",
        scatter_dimension=0,
        tiled=True,
    )
    gate_acts = summed[:, :hidden_width]
    up_acts = summed[:, hidden_width:]
    hidden = (jax.nn.silu(gate_acts) * up_acts).astype(jnp.bfloat16)
    down_local = down_weight[0]
    partial_out = jnp.dot(
        lax.all_gather(hidden, "rows", axis=0, tiled=True),
        down_local,
        preferred_element_type=jnp.float32,
    )
    block_out = lax.psum(partial_out, "hid").astype(jnp.bfloat16)
    enc_local = enc_weight[0]
    selected = block_out
    pre_rows = lax.psum_scatter(
        jnp.dot(selected, enc_local, preferred_element_type=jnp.float32),
        ("rows", "mp"),
        scatter_dimension=0,
        tiled=True,
    )
    pre_rows = pre_rows + enc_bias[None, :]
    return (jnp.maximum(pre_rows, 0.0) * adjoint.astype(jnp.float32)).astype(jnp.bfloat16)


def solution(mesh):
    placed = (
        P(("groups", "rows"), "hid"),
        P("mp", None),
        P("mp", "rows", "hid"),
        P("mp", "rows", "hid"),
        P("mp", "hid", "rows"),
        P("mp", "rows", "hid"),
        P("hid"),
        P(("groups", "rows", "mp"), "hid"),
    )
    return jax.shard_map(
        on_device,
        mesh=mesh,
        in_specs=placed,
        out_specs=P(("groups", "rows", "mp"), "hid"),
        check_vma=False,
    )
```

profile of v0, /device:TPU:0, one launch (start us, length us, event | category | flops | bytes accessed | tf_op | source)
XLA Modules:
  0.0 619.3 jit_solution(2788526948449439029)
XLA Ops:
  6.5 0.0 all-gather.4.cloned.1.call-start
  6.5 0.7 all-gather.4.cloned.1.call-update
  7.3 0.0 all-gather.6.cloned.1.call-start
  7.3 50.0 %all-gather.4.cloned.1.call-done = bf16[256,4096]{1,0:T(8,128)(2,1)} async-done(((bf16[256,1024]{1,0:T(8,128)(2,1)}), bf16[256,4096]{1,0:T(8,128)(2,1)}) %all-gather.4.cloned.1.call-update) | async-done | bytes 2097168 | tf_op jit(solution)/shard_map/all_gather | solution.py:10
  57.3 2.1 fusion.8
  59.4 3.6 fusion.10
  63.0 0.0 all-gather.6.cloned.1.call-update
  63.0 0.0 reduce-scatter.3.cloned.1.call-start
  63.1 55.6 %all-gather.6.cloned.1.call-done = bf16[512,4096]{1,0:T(8,128)(2,1)} async-done(((bf16[256,4096]{1,0:T(8,128)(2,1)}), bf16[512,4096]{1,0:T(8,128)(2,1)}) %all-gather.6.cloned.1.call-update) | async-done | bytes 4194320 | tf_op jit(solution)/shard_map/all_gather | solution.py:17
  118.7 22.1 %fusion = f32[512,7168]{1,0:T(8,128)} fusion(bf16[2048,3584]{1,0:T(8,128)(2,1)} %bitcast.12, bf16[2048,3584]{1,0:T(8,128)(2,1)} %bitcast.13, bf16[512,4096]{1,0:T(8,128)(2,1)} %all-gather.6.cloned.1.call-done, s32[]{:T(128)S(6)} %select_n.3), kind=kOutput, calls=%fused_computation | convolution fusion | flops 15091105792 | bytes 46137348 | tf_op jit(solution)/shard_map/dot_general | solution.py:24
  140.8 0.0 reduce-scatter.3.cloned.1.call-update
  140.8 0.0 all-gather.8.cloned.1.call-start
  140.9 167.3 %reduce-scatter.3.cloned.1.call-done = f32[256,7168]{1,0:T(8,128)} async-done(((f32[512,7168]{1,0:T(8,128)}), f32[256,7168]{1,0:T(8,128)}) %reduce-scatter.3.cloned.1.call-update) | async-done | bytes 7340048 | tf_op jit(solution)/shard_map/reduce_scatter | solution.py:23
  308.1 5.5 fusion.11
  313.6 0.0 all-gather.8.cloned.1.call-update
  313.6 0.0 reduce-scatter.5.cloned.1.call-start
  313.7 50.9 %all-gather.8.cloned.1.call-done = bf16[512,3584]{1,0:T(8,128)(2,1)} async-done(((bf16[256,3584]{1,0:T(8,128)(2,1)}), bf16[512,3584]{1,0:T(8,128)(2,1)}) %all-gather.8.cloned.1.call-update) | async-done | bytes 3670032 | tf_op jit(solution)/shard_map/all_gather | solution.py:34
  364.6 13.4 %fusion.6 = f32[512,2048]{1,0:T(8,128)} fusion(bf16[512,3584]{1,0:T(8,128)(2,1)} %all-gather.8.cloned.1.call-done, bf16[1,3584,2048]{2,1,0:T(8,128)(2,1)} %param.12), kind=kOutput, calls=%fused_computation.6 | convolution fusion | flops 7516192768 | bytes 22544384 | tf_op jit(solution)/shard_map/dot_general | solution.py:33
  378.0 148.0 %all-reduce.1 = bf16[512,2048]{1,0:T(8,128)(2,1)S(1)} all-reduce(f32[512,2048]{1,0:T(8,128)} %fusion.6), channel_id=1, replica_groups=mesh['groups'=2,'hid'=4,'rows'=2,'mp'=2] {'hid'}, use_global_device_ids=true, to_apply=%region_2.3 | all-reduce | flops 1048576 | bytes 6291456 | tf_op jit(solution)/shard_map/psum | solution.py:38
  526.0 14.4 %fusion.4 = f32[512,4096]{1,0:T(8,128)} fusion(bf16[1,2048,4096]{2,1,0:T(8,128)(2,1)} %param.13, bf16[512,2048]{1,0:T(8,128)(2,1)S(1)} %all-reduce.1), kind=kOutput, calls=%fused_computation.4 | convolution fusion | flops 8589934592 | bytes 27262976 | tf_op jit(solution)/shard_map/dot_general | solution.py:42
  540.4 0.0 copy-start
  540.4 0.0 copy-start.1
  540.4 0.0 reduce-scatter.5.cloned.1.call-update
  540.4 69.5 %reduce-scatter.5.cloned.1.call-done = f32[128,4096]{1,0:T(8,128)} async-done(((f32[512,4096]{1,0:T(8,128)}), f32[128,4096]{1,0:T(8,128)}) %reduce-scatter.5.cloned.1.call-update) | async-done | bytes 2097168 | tf_op jit(solution)/shard_map/reduce_scatter | solution.py:41
  609.9 0.0 copy-done
  609.9 0.0 copy-done.1
  609.9 2.9 multiply_convert_fusion
  (1 shorter events, 0.0 us)
Async XLA Ops:
  6.5 50.8 %all-gather.4.cloned.1.call-start = ((), (), s32[]{:S(2)}) async-start(), calls=%async_computation.2 | async-start | bytes 2621440 | tf_op jit(solution)/shard_map/all_gather | solution.py:10
  7.3 111.4 %all-gather.6.cloned.1.call-start = ((), (), s32[]{:S(2)}) async-start(), calls=%async_computation.3 | async-start | bytes 6291456 | tf_op jit(solution)/shard_map/all_gather | solution.py:17
  63.0 245.1 %reduce-scatter.3.cloned.1.call-start = ((), (), s32[]{:S(2)}) async-start(), calls=%async_computation.4 | async-start | bytes 22020096 | tf_op jit(solution)/shard_map/reduce_scatter | solution.py:23
  140.8 223.8 %all-gather.8.cloned.1.call-start = ((), (), s32[]{:S(2)}) async-start(), calls=%async_computation.5 | async-start | bytes 5505024 | tf_op jit(solution)/shard_map/all_gather | solution.py:34
  313.6 296.3 %reduce-scatter.5.cloned.1.call-start = ((), (), s32[]{:S(2)}) async-start(), calls=%async_computation.6 | async-start | bytes 10485760 | tf_op jit(solution)/shard_map/reduce_scatter | solution.py:41
  540.4 69.5 %copy-start = (bf16[128,4096]{1,0:T(8,128)(2,1)S(1)}, bf16[128,4096]{1,0:T(8,128)(2,1)}, u32[]{:S(2)}) copy-start(bf16[128,4096]{1,0:T(8,128)(2,1)} %param.15) | copy-start | bytes 3145732
  540.4 69.5 %copy-start.1 = (f32[4096]{0:T(1024)S(1)}, f32[4096]{0:T(1024)}, u32[]{:S(2)}) copy-start(f32[4096]{0:T(1024)} %param.14) | copy-start | bytes 49156
Sparse Core Ops, SparseCore 0:
  8.9 48.3 all-gather.3
  63.1 55.5 all-gather.5
  141.0 167.1 reduce-scatter.2
  313.7 50.8 all-gather.7
  540.5 69.3 reduce-scatter.4
where the time goes:
time: 620 us; the launch traced here: 619 us
  waiting for transfers between devices  394 us (64%)
  blocking collectives  148 us (24%)
  matrix products  49.9 us (8%)
  other arithmetic  14 us (2%)
  between operations  13.2 us (2%)
    reduce_scatter x1, waiting for transfers between devices, on_device(): lax.psum_scatter(jnp.dot(selected, both_local, preferred_element_type=jnp...  167 us
    psum x1, blocking collectives, on_device(): block_out = lax.psum(partial_out, 'hid').astype(jnp.bfloat16)  148 us
    reduce_scatter x1, waiting for transfers between devices, on_device(): lax.psum_scatter(jnp.dot(selected, enc_local, preferred_element_type=jnp....  69.5 us
    all_gather x1, waiting for transfers between devices, on_device(): all_normed = lax.all_gather(normed, 'rows', axis=0, tiled=True)  55.6 us
    all_gather x1, waiting for transfers between devices, on_device(): lax.all_gather(hidden, 'rows', axis=0, tiled=True)  50.9 us
    all_gather x1, waiting for transfers between devices, on_device(): gathered = lax.all_gather(tokens, 'hid', axis=1, tiled=True)  50 us
    dot_general x1, matrix products, on_device(): jnp.dot(selected, both_local, preferred_element_type=jnp.float32)  22.1 us
    dot_general x1, matrix products, on_device(): jnp.dot(selected, enc_local, preferred_element_type=jnp.float32)  14.4 us
  transfers between devices with their start and end apart: 5, of which 5 were waited for; matrix products, arithmetic and copies ran while one was open for 0% of the time, Pallas kernels for 0%

commit v1 on v0

--- a/solution.py
+++ b/solution.py
@@ -35,7 +35,7 @@
         down_local,
         preferred_element_type=jnp.float32,
     )
-    block_out = lax.psum(partial_out, "hid").astype(jnp.bfloat16)
+    block_out = jnp.sum(lax.all_gather(partial_out, "hid"), axis=0).astype(jnp.bfloat16)
     enc_local = enc_weight[0]
     selected = block_out
     pre_rows = lax.psum_scatter(

time: 620 us -> 767 us (1.24)
  waiting for transfers between devices: 394 us -> 681 us
  blocking collectives: 148 us -> 0 us
  other arithmetic: 14 us -> 22.1 us
    all_gather x0 -> x1, waiting for transfers between devices: none -> 287 us  [on_device(): lax.all_gather(partial_out, 'hid')]
    psum x1 -> x0, blocking collectives: 148 us -> none  [on_device(): block_out = lax.psum(partial_out, 'hid').astype(jnp.bfloat16)]
    reduce_sum x0 -> x1, other arithmetic: none -> 8.11 us  [on_device(): jnp.sum(lax.all_gather(partial_out, 'hid'), axis=0).astype(jnp.bfloat16)]
  transfers between devices with their start and end apart: 5 -> 6, of which waited for: 5 -> 6; matrix products, arithmetic and copies ran while one was open for 0% -> 0% of each run, Pallas kernels for 0% -> 0%
where the time goes in v1:
time: 767 us
  waiting for transfers between devices  681 us (89%)
  matrix products  50 us (7%)
  other arithmetic  22.1 us (3%)
  between operations  13.5 us (2%)
    all_gather x1, waiting for transfers between devices, on_device(): lax.all_gather(partial_out, 'hid')  287 us
    reduce_scatter x1, waiting for transfers between devices, on_device(): lax.psum_scatter(jnp.dot(selected, both_local, preferred_element_type=jnp...  167 us
    reduce_scatter x1, waiting for transfers between devices, on_device(): lax.psum_scatter(jnp.dot(selected, enc_local, preferred_element_type=jnp....  69.7 us
    all_gather x1, waiting for transfers between devices, on_device(): all_normed = lax.all_gather(normed, 'rows', axis=0, tiled=True)  55.6 us
    all_gather x1, waiting for transfers between devices, on_device(): lax.all_gather(hidden, 'rows', axis=0, tiled=True)  50.9 us
    all_gather x1, waiting for transfers between devices, on_device(): gathered = lax.all_gather(tokens, 'hid', axis=1, tiled=True)  50 us
    dot_general x1, matrix products, on_device(): jnp.dot(selected, both_local, preferred_element_type=jnp.float32)  22.2 us
  transfers between devices with their start and end apart: 6, of which 6 were waited for; matrix products, arithmetic and copies ran while one was open for 0% of the time, Pallas kernels for 0%

profile of v1, /device:TPU:0, one launch (start us, length us, event | category | flops | bytes accessed | tf_op | source)
XLA Modules:
  0.0 767.1 jit_solution(15519418914967437444)
XLA Ops:
  6.5 0.0 all-gather.6.cloned.1.call-start
  6.5 0.7 all-gather.6.cloned.1.call-update
  7.3 0.0 all-gather.8.cloned.1.call-start
  7.3 50.0 %all-gather.6.cloned.1.call-done = bf16[256,4096]{1,0:T(8,128)(2,1)} async-done(((bf16[256,1024]{1,0:T(8,128)(2,1)}), bf16[256,4096]{1,0:T(8,128)(2,1)}) %all-gather.6.cloned.1.call-update) | async-done | bytes 2097168 | tf_op jit(solution)/shard_map/all_gather | solution.py:10
  57.3 2.1 fusion.8
  59.4 3.6 fusion.10
  63.0 0.0 all-gather.8.cloned.1.call-update
  63.0 0.0 reduce-scatter.3.cloned.1.call-start
  63.1 55.6 %all-gather.8.cloned.1.call-done = bf16[512,4096]{1,0:T(8,128)(2,1)} async-done(((bf16[256,4096]{1,0:T(8,128)(2,1)}), bf16[512,4096]{1,0:T(8,128)(2,1)}) %all-gather.8.cloned.1.call-update) | async-done | bytes 4194320 | tf_op jit(solution)/shard_map/all_gather | solution.py:17
  118.7 22.2 %fusion = f32[512,7168]{1,0:T(8,128)} fusion(bf16[2048,3584]{1,0:T(8,128)(2,1)} %bitcast.14, bf16[2048,3584]{1,0:T(8,128)(2,1)} %bitcast.15, bf16[512,4096]{1,0:T(8,128)(2,1)} %all-gather.8.cloned.1.call-done, s32[]{:T(128)S(6)} %select_n.3), kind=kOutput, calls=%fused_computation | convolution fusion | flops 15091105792 | bytes 46137348 | tf_op jit(solution)/shard_map/dot_general | solution.py:24
  140.9 0.0 reduce-scatter.3.cloned.1.call-update
  140.9 0.0 all-gather.10.cloned.1.call-start
  141.0 167.3 %reduce-scatter.3.cloned.1.call-done = f32[256,7168]{1,0:T(8,128)} async-done(((f32[512,7168]{1,0:T(8,128)}), f32[256,7168]{1,0:T(8,128)}) %reduce-scatter.3.cloned.1.call-update) | async-done | bytes 7340048 | tf_op jit(solution)/shard_map/reduce_scatter | solution.py:23
  308.2 5.5 fusion.11
  313.7 0.0 all-gather.10.cloned.1.call-update
  313.7 0.0 all-gather.12.cloned.1.call-start
  313.8 50.9 %all-gather.10.cloned.1.call-done = bf16[512,3584]{1,0:T(8,128)(2,1)} async-done(((bf16[256,3584]{1,0:T(8,128)(2,1)}), bf16[512,3584]{1,0:T(8,128)(2,1)}) %all-gather.10.cloned.1.call-update) | async-done | bytes 3670032 | tf_op jit(solution)/shard_map/all_gather | solution.py:34
  364.7 13.5 %fusion.6 = f32[512,2048]{1,0:T(8,128)} fusion(bf16[512,3584]{1,0:T(8,128)(2,1)} %all-gather.10.cloned.1.call-done, bf16[1,3584,2048]{2,1,0:T(8,128)(2,1)} %param.12), kind=kOutput, calls=%fused_computation.6 | convolution fusion | flops 7516192768 | bytes 22544384 | tf_op jit(solution)/shard_map/dot_general | solution.py:33
  378.2 0.0 all-gather.12.cloned.1.call-update
  378.2 0.2 reduce-scatter.5.cloned.1.call-start
  378.4 286.7 %all-gather.12.cloned.1.call-done = f32[2048,2048]{1,0:T(8,128)} async-done(((f32[512,2048]{1,0:T(8,128)}), f32[2048,2048]{1,0:T(8,128)}) %all-gather.12.cloned.1.call-update) | async-done | bytes 16777232 | tf_op jit(solution)/shard_map/all_gather | solution.py:38
  665.1 8.1 %reduce_sum.19 = bf16[512,2048]{1,0:T(8,128)(2,1)S(1)} reduce(f32[4,512,2048]{2,1,0:T(8,128)} %bitcast.12, f32[]{:T(128)} %constant.8.clone.1), dimensions={0}, to_apply=%region_2.3 | reduce | flops 3145728 | bytes 18874372 | tf_op jit(solution)/shard_map/reduce_sum | solution.py:38
  673.2 14.4 %fusion.4 = f32[512,4096]{1,0:T(8,128)} fusion(bf16[1,2048,4096]{2,1,0:T(8,128)(2,1)} %param.13, bf16[512,2048]{1,0:T(8,128)(2,1)S(1)} %reduce_sum.19), kind=kOutput, calls=%fused_computation.4 | convolution fusion | flops 8589934592 | bytes 27262976 | tf_op jit(solution)/shard_map/dot_general | solution.py:42
  687.6 0.0 copy-start
  687.6 0.0 copy-start.1
  687.6 0.0 reduce-scatter.5.cloned.1.call-update
  687.6 69.7 %reduce-scatter.5.cloned.1.call-done = f32[128,4096]{1,0:T(8,128)} async-done(((f32[512,4096]{1,0:T(8,128)}), f32[128,4096]{1,0:T(8,128)}) %reduce-scatter.5.cloned.1.call-update) | async-done | bytes 2097168 | tf_op jit(solution)/shard_map/reduce_scatter | solution.py:41
  757.4 0.0 copy-done
  757.4 0.0 copy-done.1
  757.4 2.9 multiply_convert_fusion
  (1 shorter events, 0.0 us)
Async XLA Ops:
  6.5 50.8 %all-gather.6.cloned.1.call-start = ((), (), s32[]{:S(2)}) async-start(), calls=%async_computation.2 | async-start | bytes 2621440 | tf_op jit(solution)/shard_map/all_gather | solution.py:10
  7.3 111.4 %all-gather.8.cloned.1.call-start = ((), (), s32[]{:S(2)}) async-start(), calls=%async_computation.3 | async-start | bytes 6291456 | tf_op jit(solution)/shard_map/all_gather | solution.py:17
  63.0 245.2 %reduce-scatter.3.cloned.1.call-start = ((), (), s32[]{:S(2)}) async-start(), calls=%async_computation.4 | async-start | bytes 22020096 | tf_op jit(solution)/shard_map/reduce_scatter | solution.py:23
  140.9 223.8 %all-gather.10.cloned.1.call-start = ((), (), s32[]{:S(2)}) async-start(), calls=%async_computation.5 | async-start | bytes 5505024 | tf_op jit(solution)/shard_map/all_gather | solution.py:34
  313.7 351.4 %all-gather.12.cloned.1.call-start = ((), (), s32[]{:S(2)}) async-start(), calls=%async_computation.7 | async-start | bytes 20971520 | tf_op jit(solution)/shard_map/all_gather | solution.py:38
  378.2 379.2 %reduce-scatter.5.cloned.1.call-start = ((), (), s32[]{:S(2)}) async-start(), calls=%async_computation.6 | async-start | bytes 10485760 | tf_op jit(solution)/shard_map/reduce_scatter | solution.py:41
  687.6 69.8 %copy-start = (bf16[128,4096]{1,0:T(8,128)(2,1)S(1)}, bf16[128,4096]{1,0:T(8,128)(2,1)}, u32[]{:S(2)}) copy-start(bf16[128,4096]{1,0:T(8,128)(2,1)} %param.15) | copy-start | bytes 3145732
  687.6 69.8 %copy-start.1 = (f32[4096]{0:T(1024)S(1)}, f32[4096]{0:T(1024)}, u32[]{:S(2)}) copy-start(f32[4096]{0:T(1024)} %param.14) | copy-start | bytes 49156
Sparse Core Ops, SparseCore 0:
  8.9 48.3 all-gather.5
  63.1 55.5 all-gather.7
  141.0 167.1 reduce-scatter.2
  313.9 50.8 all-gather.9
  378.3 286.7 all-gather.11
  687.7 69.5 reduce-scatter.4
